TPU v7x, 32 devices: a whole 2x2x4 slice. The times are simulated.
32 devices in a mesh: space: 16 (over z, x, core), tm: 2 (over y).
Axes of the slice: x: 2, y: 2, z: 4, core: 2. Of those that a mesh axis runs over, the one named last changes fastest.
Arguments:
- thermal_anomaly: bfloat16 [128, 140288], P('tm', 'space'), may hold values from -6 to 6
- smoothing_coefs: float32 [128], replicated, may hold values from -0.0075 to 0.0075
Outputs:
- orthonormal_basis: float32 [128, 140288], P(None, ('space', 'tm'))
- triangular_factor: float32 [128, 128], replicated
All inputs are finite; a program needn't handle non-finite values.
Results may differ from a plain program's by a relative error of at most 0.0003.
The roundings to bfloat16 on the way count: a program that leaves them out, or rounds other values in their place, can miss the bound.
Values may be sent and summed in bfloat16 or wider, within the bound.
A program may use at most 64 MiB of HBM per device.

v0:
```python
import jax
import jax.numpy as jnp
from jax import lax
from jax.sharding import PartitionSpec as P


def shifted(block, axis, distance):
    devices = range(lax.axis_size(axis))
    route = [(i - distance, i) for i in devices if i - distance in devices]
    return lax.ppermute(block, axis, route)


def banded_matrix(coefficients, count_rows, count_cols, delay_shift_amount):
    row_index = lax.broadcasted_iota(jnp.int32, (count_rows, count_cols), 0)
    col_index = lax.broadcasted_iota(jnp.int32, (count_rows, count_cols), 1)
    lag_index = row_index + delay_shift_amount - col_index
    length = coefficients.shape[0]
    inside = (lag_index >= 0) & (lag_index < length)
    safe = jnp.clip(lag_index, 0, length - 1)
    return jnp.where(inside, coefficients[safe], jnp.zeros((), coefficients.dtype))


def product_low(left, right):
    return jnp.dot(left, right.T, preferred_element_type=jnp.float32)


def summed_gram(panel):
    width_block = panel.shape[0] // 4
    pieces = [panel[index * width_block : (index + 1) * width_block] for index in range(4)]
    listing = []
    for row_block in range(4):
        for col_block in range(row_block + 1):
            listing.append(product_low(pieces[row_block], pieces[col_block]))
    stacked = lax.psum(jnp.stack(listing), ("space", "tm"))
    lookup = {}
    position = 0
    for row_block in range(4):
        for col_block in range(row_block + 1):
            lookup[row_block, col_block] = stacked[position]
            position = position + 1
    band_rows = []
    for row_block in range(4):
        entries = []
        for col_block in range(4):
            if col_block <= row_block:
                entries.append(lookup[row_block, col_block])
            else:
                entries.append(lookup[col_block, row_block].T)
        band_rows.append(jnp.concatenate(entries, axis=1))
    return jnp.concatenate(band_rows, axis=0)


def body(thermal_anomaly, smoothing_coefs):
    timesteps_each_shard = thermal_anomaly.shape[0]
    coefficients = jnp.concatenate([jnp.ones((1,), jnp.float32), smoothing_coefs]).astype(
        jnp.bfloat16
    )
    prior_timesteps = []
    for delay_shift_amount in (2, 1):
        prior_timesteps.append(shifted(thermal_anomaly, "tm", delay_shift_amount))
    extended_record = jnp.concatenate(prior_timesteps + [thermal_anomaly], axis=0)
    snapshot_array = banded_matrix(
        coefficients, timesteps_each_shard, 3 * timesteps_each_shard, 2 * timesteps_each_shard
    )
    outgoing = jnp.dot(snapshot_array, extended_record, preferred_element_type=jnp.float32).astype(
        jnp.bfloat16
    )
    arrived = lax.all_to_all(outgoing, "tm", split_axis=1, concat_axis=0, tiled=True)
    gram = summed_gram(arrived)
    lower_one = jnp.linalg.cholesky(gram)
    first_rows = jax.scipy.linalg.solve_triangular(
        lower_one, arrived.astype(jnp.float32), lower=True
    )
    location_total = thermal_anomaly.shape[1] * lax.axis_size("space")
    scale = jnp.sqrt(jnp.float32(location_total))
    return (first_rows * scale, lower_one / scale)


def solution(mesh):
    placed = (P("tm", "space"), P())
    return jax.shard_map(
        body, mesh=mesh, in_specs=placed, out_specs=(P(None, ("space", "tm")), P()), check_vma=False
    )
```

profile of v0, /device:TPU:0, one launch (start us, length us, event | category | flops | bytes accessed | tf_op | source)
XLA Modules:
  0.0 173.4 jit_solution(4869511577980264260)
XLA Ops:
  0.6 0.7 collective-permute-start
  1.4 5.9 %collective-permute-start.1 = (bf16[64,8768]{1,0:T(8,128)(2,1)}, bf16[64,8768]{1,0:T(8,128)(2,1)}, u32[]{:S(2)}, u32[]{:S(2)}) collective-permute-start(bf16[64,8768]{1,0:T(8,128)(2,1)} %param.2), channel_id=1, source_target_pairs={{0,1},{2,3},{4,5},{6,7},{8,9},{10,11},{12,13},{14,15},{16,17},{18,... | collective-permute-start | bytes 3366920 | tf_op jit(solution)/shard_map/ppermute | solution.py:10
  7.3 0.7 convert.4
  8.0 0.1 reshape.58
  8.2 72.2 %gather_fusion = bf16[12288]{0:T(1024)(128)(2,1)S(1)} fusion(bf16[129]{0:T(256)(128)(2,1)S(1)} %pad_maximum_fusion.2, s32[12288]{0:T(1024)S(1)} %broadcast_clamp_fusion), kind=kCustom, calls=%fused_computation | custom fusion | bytes 98304 | tf_op jit(solution)/shard_map/gather | solution.py:20
  80.4 0.1 reshape.57
  80.5 2.1 %convolution_convert_fusion = bf16[64,8768]{1,0:T(8,128)(2,1)S(1)} fusion(bf16[64,8768]{1,0:T(8,128)(2,1)S(1)} %copy-done, bf16[64,8768]{1,0:T(8,128)(2,1)} %collective-permute-done.1, bf16[64,8768]{1,0:T(8,128)(2,1)S(1)} %collective-permute-done, bf16[64,192]{1,0:T(8,128)(2,1)S(1)} %reshape.57, s32[64]{0:T(128)S(1)} %iota_add_fusion), kind=kOutput, calls=%fused_computation.1 | convolution fusion | flops 226205696 | bytes 4514048 | tf_op jit(solution)/shard_map/dot_general | solution.py:65
  82.6 1.2 all_to_all.14
  83.8 0.1 copy.76
  84.0 17.1 %all_to_all.19 = bf16[64,2,4384]{2,0,1:T(8,128)(2,1)S(1)} all-to-all(bf16[64,2,4384]{2,0,1:T(8,128)(2,1)S(1)} %copy.76), channel_id=1, replica_groups=mesh['space'=16,'tm'=2] {'tm'}, dimensions={1} | all-to-all | bytes 2244608 | tf_op jit(solution)/shard_map/all_to_all | solution.py:68
  101.1 0.2 fusion.14
  101.3 0.2 fusion.13
  101.5 0.2 fusion.12
  101.7 0.2 fusion.11
  101.9 0.2 fusion.10
  102.1 0.2 fusion.9
  102.4 0.2 fusion.8
  102.6 0.2 fusion.7
  102.8 0.2 fusion.6
  103.0 0.2 fusion.5
  103.3 42.9 %psum.7 = f32[10,32,32]{1,2,0:T(8,128)S(1)} all-reduce(f32[10,32,32]{1,2,0:T(8,128)S(1)} %fusion.5), channel_id=1, replica_groups=mesh['space'=16,'tm'=2] {'space','tm'}, use_global_device_ids=true, to_apply=%region_0.1 | all-reduce | flops 10240 | bytes 81920 | tf_op jit(solution)/shard_map/psum | solution.py:34
  146.5 0.1 pad_maximum_fusion
  146.6 0.1 copy.93
  146.7 0.1 copy.94
  146.8 0.1 maximum_maximum_fusion
  147.0 0.1 copy.95
  147.1 0.1 fusion.32
  147.2 11.7 %cholesky.16 = f32[128,128]{1,0:T(8,128)S(1)} custom-call(f32[128,128]{1,0:T(8,128)S(1)} %fusion.32), custom_call_target="Cholesky" | custom-call | tf_op jit(solution)/shard_map/jit(cholesky)/cholesky | solution.py:70
  158.9 0.6 compare_reduce_fusion
  159.6 1.3 fusion.37
  160.9 9.8 %custom-call.7 = f32[1,128,128]{1,2,0:T(8,128)S(1)} custom-call(f32[1,128,128]{2,1,0:T(8,128)S(1)} %get-tuple-element.18), custom_call_target="InvertDiagBlocksLowerTriangular" | custom-call | tf_op jit(solution)/shard_map/jit(_solve_triangular)/triangular_solve | solution.py:71
  170.7 2.7 %convolution_multiply_fusion = f32[128,4384]{0,1:T(8,128)} fusion(bf16[128,4384]{1,0:T(8,128)(2,1)S(1)} %bitcast.99, f32[1,128,128]{1,2,0:T(8,128)S(1)} %custom-call.7), kind=kOutput, calls=%fused_computation.2 | convolution fusion | flops 862490624 | bytes 3432448 | tf_op jit(solution)/shard_map/jit(_solve_triangular)/triangular_solve | solution.py:71
  (15 shorter events, 0.6 us)
Async XLA Ops:
  0.6 79.9 %collective-permute-start = (bf16[64,8768]{1,0:T(8,128)(2,1)}, bf16[64,8768]{1,0:T(8,128)(2,1)S(1)}, u32[]{:S(2)}, u32[]{:S(2)}) collective-permute-start(bf16[64,8768]{1,0:T(8,128)(2,1)} %param.2), channel_id=1, source_target_pairs={} | collective-permute-start | bytes 3366920 | tf_op jit(solution)/shard_map/ppermute | solution.py:10
  1.4 79.1 %collective-permute-start.1 = (bf16[64,8768]{1,0:T(8,128)(2,1)}, bf16[64,8768]{1,0:T(8,128)(2,1)}, u32[]{:S(2)}, u32[]{:S(2)}) collective-permute-start(bf16[64,8768]{1,0:T(8,128)(2,1)} %param.2), channel_id=1, source_target_pairs={{0,1},{2,3},{4,5},{6,7},{8,9},{10,11},{12,13},{14,15},{16,17},{18,... | collective-permute-start | bytes 3366920 | tf_op jit(solution)/shard_map/ppermute | solution.py:10
  8.2 72.3 %copy-start = (bf16[64,8768]{1,0:T(8,128)(2,1)S(1)}, bf16[64,8768]{1,0:T(8,128)(2,1)}, u32[]{:S(2)}) copy-start(bf16[64,8768]{1,0:T(8,128)(2,1)} %param.2) | copy-start | bytes 3366916
where the time goes:
time: 174 us; the launch traced here: 173 us
  local copies, waits for them, and re-layouts  74.4 us (43%)
  blocking collectives  60 us (34%)
  other arithmetic  24.7 us (14%)
  matrix products  6.89 us (4%)
  starting transfers between devices  6.63 us (4%)
    gather x2, local copies, waits for them, and re-layouts, banded_matrix(): coefficients[safe]  72.3 us
    psum x1, blocking collectives, summed_gram(): stacked = lax.psum(jnp.stack(listing), ('space', 'tm'))  42.9 us
    all_to_all x1, blocking collectives, body(): lax.all_to_all(outgoing, 'tm', split_axis=1, concat_axis=0, tiled=True)  17.1 us
    another operation x3, other arithmetic, body(): lower_one = jnp.linalg.cholesky(gram)  12.4 us
    another operation x1, other arithmetic, body(): jax.scipy.linalg.solve_triangular(lower_one, arrived.astype(jnp.float32),...  9.81 us
    ppermute x2, starting transfers between devices, shifted(): return lax.ppermute(block, axis, route)  6.63 us
  transfers between devices with their start and end apart: 2, of which 0 were waited for; matrix products, arithmetic and copies ran while one was open for 42% of the time, Pallas kernels for 0%

commit v1 on v0

--- a/solution.py
+++ b/solution.py
@@ -65,7 +65,10 @@
     outgoing = jnp.dot(snapshot_array, extended_record, preferred_element_type=jnp.float32).astype(
         jnp.bfloat16
     )
-    arrived = lax.all_to_all(outgoing, "tm", split_axis=1, concat_axis=0, tiled=True)
+    arrived = jnp.concatenate(
+        lax.all_to_all(jnp.stack(jnp.split(outgoing, lax.axis_size("tm"), axis=1)), "tm", 0, 0),
+        axis=0,
+    )
     gram = summed_gram(arrived)
     lower_one = jnp.linalg.cholesky(gram)
     first_rows = jax.scipy.linalg.solve_triangular(

time: 174 us -> 170 us (0.977)
  transfers between devices with their start and end apart: 2 -> 2, of which waited for: 0 -> 0; matrix products, arithmetic and copies ran while one was open for 42% -> 43% of each run, Pallas kernels for 0% -> 0%
where the time goes in v1:
time: 170 us
  local copies, waits for them, and re-layouts  73.3 us (43%)
  blocking collectives  59.9 us (35%)
  other arithmetic  24.8 us (15%)
  starting transfers between devices  5.7 us (3%)
  matrix products  5.63 us (3%)
    gather x2, local copies, waits for them, and re-layouts, banded_matrix(): coefficients[safe]  72.3 us
    psum x1, blocking collectives, summed_gram(): stacked = lax.psum(jnp.stack(listing), ('space', 'tm'))  42.9 us
    all_to_all x1, blocking collectives, body(): lax.all_to_all(jnp.stack(jnp.split(outgoing, lax.axis_size('tm'), axis=1)...  17.1 us
    another operation x3, other arithmetic, body(): lower_one = jnp.linalg.cholesky(gram)  12.4 us
    another operation x1, other arithmetic, body(): jax.scipy.linalg.solve_triangular(lower_one, arrived.astype(jnp.float32),...  9.81 us
    ppermute x2, starting transfers between devices, shifted(): return lax.ppermute(block, axis, route)  5.7 us
  transfers between devices with their start and end apart: 2, of which 0 were waited for; matrix products, arithmetic and copies ran while one was open for 43% of the time, Pallas kernels for 0%

profile of v1, /device:TPU:0, one launch (start us, length us, event | category | flops | bytes accessed | tf_op | source)
XLA Modules:
  0.0 170.2 jit_solution(11029027334082231849)
XLA Ops:
  0.6 0.7 collective-permute-start
  1.4 5.0 %collective-permute-start.1 = (bf16[64,8768]{1,0:T(8,128)(2,1)}, bf16[64,8768]{1,0:T(8,128)(2,1)S(1)}, u32[]{:S(2)}, u32[]{:S(2)}) collective-permute-start(bf16[64,8768]{1,0:T(8,128)(2,1)} %param.2), channel_id=1, source_target_pairs={{0,1},{2,3},{4,5},{6,7},{8,9},{10,11},{12,13},{14,15},{16,17},{18,... | collective-permute-start | bytes 3366920 | tf_op jit(solution)/shard_map/ppermute | solution.py:10
  6.3 0.7 convert.4
  7.1 0.1 reshape.59
  7.3 72.2 %gather_fusion = bf16[12288]{0:T(1024)(128)(2,1)S(1)} fusion(bf16[129]{0:T(256)(128)(2,1)S(1)} %pad_maximum_fusion.3, s32[12288]{0:T(1024)S(1)} %broadcast_clamp_fusion), kind=kCustom, calls=%fused_computation | custom fusion | bytes 98304 | tf_op jit(solution)/shard_map/gather | solution.py:20
  79.5 0.1 reshape.58
  79.6 0.8 convolution_convert_fusion
  80.4 0.2 slice_bitcast_fusion.1
  80.7 0.1 pad_maximum_fusion
  80.8 17.1 %all_to_all.5 = bf16[2,64,4384]{2,1,0:T(8,128)(2,1)S(1)} all-to-all(bf16[2,64,4384]{2,1,0:T(8,128)(2,1)S(1)} %pad_maximum_fusion), channel_id=1, replica_groups=mesh['space'=16,'tm'=2] {'tm'}, dimensions={0} | all-to-all | bytes 2244608 | tf_op jit(solution)/shard_map/all_to_all | solution.py:69
  97.9 0.2 fusion.14
  98.1 0.2 fusion.13
  98.3 0.2 fusion.12
  98.5 0.2 fusion.11
  98.7 0.2 fusion.10
  99.0 0.2 fusion.9
  99.2 0.2 fusion.8
  99.4 0.2 fusion.7
  99.6 0.2 fusion.6
  99.8 0.2 fusion.5
  100.1 42.9 %psum.7 = f32[10,32,32]{1,2,0:T(8,128)S(1)} all-reduce(f32[10,32,32]{1,2,0:T(8,128)S(1)} %fusion.5), channel_id=1, replica_groups=mesh['space'=16,'tm'=2] {'space','tm'}, use_global_device_ids=true, to_apply=%region_0.1 | all-reduce | flops 10240 | bytes 81920 | tf_op jit(solution)/shard_map/psum | solution.py:34
  143.3 0.1 pad_maximum_fusion.1
  143.4 0.1 copy.88
  143.5 0.1 copy.89
  143.6 0.1 maximum_maximum_fusion
  143.8 0.1 copy.90
  143.9 0.1 fusion.32
  144.0 11.7 %cholesky.16 = f32[128,128]{1,0:T(8,128)S(1)} custom-call(f32[128,128]{1,0:T(8,128)S(1)} %fusion.32), custom_call_target="Cholesky" | custom-call | tf_op jit(solution)/shard_map/jit(cholesky)/cholesky | solution.py:73
  155.7 0.6 compare_reduce_fusion
  156.4 1.3 fusion.37
  157.7 9.8 %custom-call.7 = f32[1,128,128]{1,2,0:T(8,128)S(1)} custom-call(f32[1,128,128]{2,1,0:T(8,128)S(1)} %get-tuple-element.20), custom_call_target="InvertDiagBlocksLowerTriangular" | custom-call | tf_op jit(solution)/shard_map/jit(_solve_triangular)/triangular_solve | solution.py:74
  167.5 2.7 %convolution_multiply_fusion = f32[128,4384]{0,1:T(8,128)} fusion(bf16[128,4384]{1,0:T(8,128)(2,1)S(1)} %bitcast.101, f32[1,128,128]{1,2,0:T(8,128)S(1)} %custom-call.7), kind=kOutput, calls=%fused_computation.2 | convolution fusion | flops 862490624 | bytes 3432448 | tf_op jit(solution)/shard_map/jit(_solve_triangular)/triangular_solve | solution.py:74
  (15 shorter events, 0.6 us)
Async XLA Ops:
  0.6 79.0 %collective-permute-start = (bf16[64,8768]{1,0:T(8,128)(2,1)}, bf16[64,8768]{1,0:T(8,128)(2,1)S(1)}, u32[]{:S(2)}, u32[]{:S(2)}) collective-permute-start(bf16[64,8768]{1,0:T(8,128)(2,1)} %param.2), channel_id=1, source_target_pairs={} | collective-permute-start | bytes 3366920 | tf_op jit(solution)/shard_map/ppermute | solution.py:10
  1.4 78.2 %collective-permute-start.1 = (bf16[64,8768]{1,0:T(8,128)(2,1)}, bf16[64,8768]{1,0:T(8,128)(2,1)S(1)}, u32[]{:S(2)}, u32[]{:S(2)}) collective-permute-start(bf16[64,8768]{1,0:T(8,128)(2,1)} %param.2), channel_id=1, source_target_pairs={{0,1},{2,3},{4,5},{6,7},{8,9},{10,11},{12,13},{14,15},{16,17},{18,... | collective-permute-start | bytes 3366920 | tf_op jit(solution)/shard_map/ppermute | solution.py:10
  7.3 72.3 %copy-start = (bf16[64,8768]{1,0:T(8,128)(2,1)S(1)}, bf16[64,8768]{1,0:T(8,128)(2,1)}, u32[]{:S(2)}) copy-start(bf16[64,8768]{1,0:T(8,128)(2,1)} %param.2) | copy-start | bytes 3366916
